TPU v7x, 32 devices: a whole 2x2x4 slice. The times are simulated.
32 devices in a mesh: dp: 8 (over y, x, core), group: 4 (over z).
Axes of the slice: x: 2, y: 2, z: 4, core: 2. Of those that a mesh axis runs over, the one named last changes fastest.
Arguments:
- inputs: float32 [4096, 768], P(('dp', 'group')), may hold values from -6 to 6
- cotangent: float32 [4096, 768], P(('dp', 'group')), may hold values from -6 to 6
- lengths: int32 [32, 4], P(('dp', 'group')), may hold values from 1 to 64, 128 in all within a row
- attn_weights: float32 [4, 768, 768], P('group', 'dp'), may hold values from -1 to 1
- attn_momenta: float32 [4, 768, 768], P('group', 'dp'), may hold values from -1 to 1
- ffn_weights: float32 [2, 768, 3072], P(None, 'dp', 'group'), may hold values from -1 to 1
- ffn_momenta: float32 [2, 768, 3072], P(None, 'dp', 'group'), may hold values from -1 to 1
- vectors: float32 [12, 768], replicated, may hold values from -2 to 2
- vector_momenta: float32 [12, 768], replicated, may hold values from -1 to 1
Outputs:
- outputs: float32 [4096, 768], P(('dp', 'group'))
- input_grad: float32 [4096, 768], P(('dp', 'group'))
- attn_grads: float32 [4, 768, 768], P('group', 'dp')
- ffn_grads: float32 [2, 768, 3072], P(None, 'dp', 'group')
- vector_grads: float32 [12, 768], replicated
- new_attn_weights: float32 [4, 768, 768], P('group', 'dp')
- new_attn_momenta: float32 [4, 768, 768], P('group', 'dp')
- new_ffn_weights: float32 [2, 768, 3072], P(None, 'dp', 'group')
- new_ffn_momenta: float32 [2, 768, 3072], P(None, 'dp', 'group')
- new_vectors: float32 [12, 768], replicated
- new_vector_momenta: float32 [12, 768], replicated
Inputs may be any that keep to these rules, and one draw needn't show every extreme that they name: Each device's 4 lengths sum to 128.
All inputs are finite; a program needn't handle non-finite values.
Results may differ from a plain program's by a relative error of at most 0.025.
The roundings to bfloat16 on the way count: a program that leaves them out, or rounds other values in their place, can miss the bound.
Values may be sent and summed in bfloat16 or wider, within the bound.
A program may use at most 128 MiB of HBM per device.

v0:
```python
import math
import jax
import jax.numpy as jnp
from jax import lax
from jax.sharding import PartitionSpec as P

HEADS = 12
NS_ITERS = 3
coef_first = 3.4445
coef_second = -4.775
coef_third = 2.0315
momentum_rate = 0.9
muon_rate = 0.8
vector_rate = 0.1


def norm_forward(rows):
    centre = jnp.mean(rows, axis=1, keepdims=True)
    centred = rows - centre
    variance = jnp.mean(centred * centred, axis=1, keepdims=True)
    inverse = lax.rsqrt(variance + 1e-05)
    return (centred * inverse, inverse)


def norm_backward(grad_normed, normed, inverse):
    return inverse * (
        grad_normed
        - jnp.mean(grad_normed, axis=1, keepdims=True)
        - normed * jnp.mean(grad_normed * normed, axis=1, keepdims=True)
    )


def masked_scores(query_heads, key_heads, allowed):
    scores = jnp.einsum("qhd,khd->hqk", query_heads, key_heads, preferred_element_type=jnp.float32)
    return jnp.where(allowed[None], scores, -jnp.inf)


def layer_block(block_rows, block_cotan, seq_lengths, attn_w, ffn_w, vectors):
    token_count = block_rows.shape[0]
    width = block_rows.shape[1]
    head_size = width // HEADS
    scale = 1.0 / math.sqrt(head_size)
    w_query, w_key, w_value, w_output = (attn_w[0], attn_w[1], attn_w[2], attn_w[3])
    w_expand, w_reduce = (ffn_w[0], ffn_w[1])
    expand_bias = vectors[8:].reshape(-1)
    positions = jnp.arange(token_count, dtype=jnp.int32)
    seq_ends = jnp.cumsum(seq_lengths)
    segment = jnp.sum((positions[:, None] >= seq_ends[None, :]).astype(jnp.int32), axis=1)
    allowed = (segment[:, None] == segment[None, :]) & (positions[None, :] <= positions[:, None])
    normed_first, inverse_first = norm_forward(block_rows)
    hidden_first = (normed_first * vectors[0] + vectors[1]).astype(jnp.bfloat16)
    query = (
        (jnp.dot(hidden_first, w_query, preferred_element_type=jnp.float32) + vectors[2]) * scale
    ).astype(jnp.bfloat16)
    keyed = jnp.dot(hidden_first, w_key, preferred_element_type=jnp.float32).astype(jnp.bfloat16)
    valued = (
        jnp.dot(hidden_first, w_value, preferred_element_type=jnp.float32) + vectors[3]
    ).astype(jnp.bfloat16)
    query_heads = query.reshape(token_count, HEADS, head_size)
    key_heads = keyed.reshape(token_count, HEADS, head_size)
    value_heads = valued.reshape(token_count, HEADS, head_size)
    scores = masked_scores(query_heads, key_heads, allowed)
    highest = jnp.max(scores, axis=2, keepdims=True)
    log_total = highest + jnp.log(jnp.sum(jnp.exp(scores - highest), axis=2, keepdims=True))
    probs_first = jnp.exp(scores - log_total).astype(jnp.bfloat16)
    attended = jnp.einsum(
        "hqk,khd->qhd", probs_first, value_heads, preferred_element_type=jnp.float32
    )
    attended = attended.reshape(token_count, width).astype(jnp.bfloat16)
    middle = (
        block_rows + jnp.dot(attended, w_output, preferred_element_type=jnp.float32) + vectors[4]
    )
    normed_second, inverse_second = norm_forward(middle)
    hidden_second = (normed_second * vectors[5] + vectors[6]).astype(jnp.bfloat16)
    before = jnp.dot(hidden_second, w_expand, preferred_element_type=jnp.float32) + expand_bias
    active = jnp.maximum(before, 0.0).astype(jnp.bfloat16)
    outputs = (
        middle
        + jnp.einsum("tf,df->td", active, w_reduce, preferred_element_type=jnp.float32)
        + vectors[7]
    )
    cotan_b = block_cotan.astype(jnp.bfloat16)
    grad_active = jnp.dot(cotan_b, w_reduce, preferred_element_type=jnp.float32)
    grad_before = jnp.where(before > 0.0, grad_active, 0.0)
    before_grad_b = grad_before.astype(jnp.bfloat16)
    grad_second = jnp.einsum(
        "tf,cf->tc", before_grad_b, w_expand, preferred_element_type=jnp.float32
    )
    grad_middle = block_cotan + norm_backward(
        grad_second * vectors[5], normed_second, inverse_second
    )
    middle_b = grad_middle.astype(jnp.bfloat16)
    grad_attended = jnp.einsum(
        "td,cd->tc", middle_b, w_output, preferred_element_type=jnp.float32
    ).astype(jnp.bfloat16)
    attended_heads = grad_attended.reshape(token_count, HEADS, head_size)
    probs = jnp.exp(masked_scores(query_heads, key_heads, allowed) - log_total)
    probs_b = probs.astype(jnp.bfloat16)
    grad_probs = jnp.einsum(
        "qhd,khd->hqk", attended_heads, value_heads, preferred_element_type=jnp.float32
    )
    grad_value = jnp.einsum(
        "hqk,qhd->khd", probs_b, attended_heads, preferred_element_type=jnp.float32
    )
    delta = jnp.sum(probs * grad_probs, axis=2, keepdims=True)
    grad_scores = (probs * (grad_probs - delta)).astype(jnp.bfloat16)
    grad_query = (
        jnp.einsum("hqk,khd->qhd", grad_scores, key_heads, preferred_element_type=jnp.float32)
        * scale
    )
    grad_key = jnp.einsum(
        "hqk,qhd->khd", grad_scores, query_heads, preferred_element_type=jnp.float32
    )
    query_grad = grad_query.reshape(token_count, width)
    key_grad = grad_key.reshape(token_count, width)
    value_grad = grad_value.reshape(token_count, width)
    query_grad_b = query_grad.astype(jnp.bfloat16)
    key_grad_b = key_grad.astype(jnp.bfloat16)
    value_grad_b = value_grad.astype(jnp.bfloat16)
    grad_first = jnp.einsum("td,cd->tc", query_grad_b, w_query, preferred_element_type=jnp.float32)
    grad_first = grad_first + jnp.einsum(
        "td,cd->tc", key_grad_b, w_key, preferred_element_type=jnp.float32
    )
    grad_first = grad_first + jnp.einsum(
        "td,cd->tc", value_grad_b, w_value, preferred_element_type=jnp.float32
    )
    input_grad = grad_middle + norm_backward(grad_first * vectors[0], normed_first, inverse_first)
    small_terms = jnp.stack(
        [
            jnp.sum(grad_first * normed_first, axis=0),
            jnp.sum(grad_first, axis=0),
            jnp.sum(query_grad, axis=0),
            jnp.sum(value_grad, axis=0),
            jnp.sum(grad_middle, axis=0),
            jnp.sum(grad_second * normed_second, axis=0),
            jnp.sum(grad_second, axis=0),
            jnp.sum(block_cotan, axis=0),
        ]
    )
    bias_terms = jnp.sum(grad_before, axis=0).reshape(-1, width)
    vector_terms = jnp.concatenate([small_terms, bias_terms], axis=0)
    pieces = (
        hidden_first,
        attended,
        query_grad_b,
        key_grad_b,
        value_grad_b,
        middle_b,
        hidden_second,
        cotan_b,
        before_grad_b,
        active,
    )
    return (outputs, input_grad, vector_terms, pieces)


def owned_terms(pieces):
    group_count = lax.axis_size("group")
    own_index = lax.axis_index("group")
    (
        hidden_first,
        attended,
        query_grad_b,
        key_grad_b,
        value_grad_b,
        middle_b,
        hidden_second,
        cotan_b,
        before_grad_b,
        active,
    ) = pieces
    quarter = before_grad_b.shape[1] // group_count
    gathered = (
        lax.all_gather(hidden_first, "group", axis=0, tiled=True),
        lax.all_gather(attended, "group", axis=0, tiled=True),
        lax.all_gather(query_grad_b, "group", axis=0, tiled=True),
        lax.all_gather(key_grad_b, "group", axis=0, tiled=True),
        lax.all_gather(value_grad_b, "group", axis=0, tiled=True),
        lax.all_gather(middle_b, "group", axis=0, tiled=True),
        lax.all_gather(hidden_second, "group", axis=0, tiled=True),
        lax.all_gather(cotan_b, "group", axis=0, tiled=True),
        lax.all_gather(before_grad_b, "group", axis=0, tiled=True),
        lax.all_gather(active, "group", axis=0, tiled=True),
    )
    (
        all_first,
        all_attended,
        all_query,
        all_key,
        all_value,
        all_middle,
        all_second,
        all_cotan,
        all_before,
        all_active,
    ) = gathered
    left_side = jnp.where(own_index == 3, all_attended, all_first)
    right_stack = jnp.stack([all_query, all_key, all_value, all_middle])
    right_side = lax.dynamic_index_in_dim(right_stack, own_index, 0, keepdims=False)
    before_part = lax.dynamic_slice_in_dim(all_before, own_index * quarter, quarter, 1)
    active_part = lax.dynamic_slice_in_dim(all_active, own_index * quarter, quarter, 1)
    attn_term = jnp.einsum("tc,td->cd", left_side, right_side, preferred_element_type=jnp.float32)
    ffn_term = jnp.stack(
        [
            jnp.einsum("tc,tf->cf", all_second, before_part, preferred_element_type=jnp.float32),
            jnp.einsum("td,tf->df", all_cotan, active_part, preferred_element_type=jnp.float32),
        ]
    )
    return (attn_term, ffn_term)


def orthogonalize_rows(attn_rows, ffn_rows, attn_square, ffn_square):
    attn_iter = attn_rows / (jnp.sqrt(attn_square) + 1e-07)
    ffn_iter = ffn_rows / (jnp.sqrt(ffn_square)[:, None, None] + 1e-07)
    for iteration in range(NS_ITERS):
        attn_iter_b = attn_iter.astype(jnp.bfloat16)
        ffn_iter_b = ffn_iter.astype(jnp.bfloat16)
        attn_full, ffn_full = (
            lax.all_gather(attn_iter_b, "dp", axis=0, tiled=True),
            lax.all_gather(ffn_iter_b, "dp", axis=1, tiled=True),
        )
        attn_gram = jnp.einsum(
            "ik,jk->ij", attn_iter_b, attn_full, preferred_element_type=jnp.float32
        )
        ffn_part = jnp.einsum(
            "mik,mjk->mij", ffn_iter_b, ffn_full, preferred_element_type=jnp.float32
        )
        ffn_gram = lax.psum(ffn_part, "group")
        attn_gram_b = attn_gram.astype(jnp.bfloat16)
        ffn_gram_b = ffn_gram.astype(jnp.bfloat16)
        attn_gram_full, ffn_gram_full = (
            lax.all_gather(attn_gram_b, "dp", axis=0, tiled=True),
            lax.all_gather(ffn_gram_b, "dp", axis=1, tiled=True),
        )
        attn_mixed = coef_second * attn_gram + coef_third * jnp.dot(
            attn_gram_b, attn_gram_full, preferred_element_type=jnp.float32
        )
        ffn_mixed = coef_second * ffn_gram + coef_third * jnp.einsum(
            "mik,mkj->mij", ffn_gram_b, ffn_gram_full, preferred_element_type=jnp.float32
        )
        attn_iter = coef_first * attn_iter + jnp.dot(
            attn_mixed.astype(jnp.bfloat16), attn_full, preferred_element_type=jnp.float32
        )
        ffn_iter = coef_first * ffn_iter + jnp.einsum(
            "mik,mkj->mij",
            ffn_mixed.astype(jnp.bfloat16),
            ffn_full,
            preferred_element_type=jnp.float32,
        )
    return (attn_iter, ffn_iter)


def on_device(
    inputs,
    cotangent,
    lengths,
    attn_weights,
    attn_momenta,
    ffn_weights,
    ffn_momenta,
    vectors,
    vector_momenta,
):
    own_attn = attn_weights.astype(jnp.bfloat16)
    own_ffn = ffn_weights.astype(jnp.bfloat16)
    attn_rows, ffn_rows = (
        lax.all_gather(own_attn, "dp", axis=1, tiled=True),
        lax.all_gather(own_ffn, "dp", axis=1, tiled=True),
    )
    attn_whole, ffn_whole = (
        lax.all_gather(attn_rows, "group", axis=0, tiled=True),
        lax.all_gather(ffn_rows, "group", axis=2, tiled=True),
    )
    outputs, input_grad, vector_terms, pieces = layer_block(
        inputs, cotangent, lengths[0], attn_whole, ffn_whole, vectors
    )
    attn_term, ffn_term = owned_terms(pieces)
    attn_total, ffn_total = (
        lax.psum_scatter(attn_term, "dp", scatter_dimension=0, tiled=True),
        lax.psum_scatter(ffn_term, "dp", scatter_dimension=1, tiled=True),
    )
    group_count = lax.axis_size("group")
    total_tokens = float(inputs.shape[0] * lax.axis_size("dp") * group_count)
    attn_grads = attn_total[None] / total_tokens
    ffn_grads = ffn_total / total_tokens
    attn_next = momentum_rate * attn_momenta + attn_grads
    ffn_next = momentum_rate * ffn_momenta + ffn_grads
    owner_mask = (jnp.arange(group_count, dtype=jnp.int32) == lax.axis_index("group")).astype(
        jnp.float32
    )
    square_terms = jnp.concatenate(
        [owner_mask * jnp.sum(attn_next * attn_next), jnp.sum(ffn_next * ffn_next, axis=(1, 2))]
    )
    vector_total, square_total = lax.psum((vector_terms, square_terms), ("dp", "group"))
    attn_square = jnp.sum(square_total[:group_count] * owner_mask)
    ffn_square = square_total[group_count:]
    attn_step, ffn_step = orthogonalize_rows(attn_next[0], ffn_next, attn_square, ffn_square)
    new_attn_weights = attn_weights - muon_rate * attn_step[None]
    new_ffn_weights = ffn_weights - muon_rate * ffn_step
    vector_grads = vector_total / total_tokens
    new_vector_momenta = momentum_rate * vector_momenta + vector_grads
    spread = lax.rsqrt(
        jnp.mean(new_vector_momenta * new_vector_momenta, axis=1, keepdims=True) + 1e-06
    )
    new_vectors = vectors - vector_rate * new_vector_momenta * spread
    return (
        outputs,
        input_grad,
        attn_grads,
        ffn_grads,
        vector_grads,
        new_attn_weights,
        attn_next,
        new_ffn_weights,
        ffn_next,
        new_vectors,
        new_vector_momenta,
    )


def solution(mesh):
    in_specs = (
        P(("dp", "group"), None),
        P(("dp", "group"), None),
        P(("dp", "group"), None),
        P("group", "dp", None),
        P("group", "dp", None),
        P(None, "dp", "group"),
        P(None, "dp", "group"),
        P(),
        P(),
    )
    out_specs = (
        P(("dp", "group"), None),
        P(("dp", "group"), None),
        P("group", "dp", None),
        P(None, "dp", "group"),
        P(),
        P("group", "dp", None),
        P("group", "dp", None),
        P(None, "dp", "group"),
        P(None, "dp", "group"),
        P(),
        P(),
    )
    return jax.shard_map(
        on_device, mesh=mesh, in_specs=in_specs, out_specs=out_specs, check_vma=False
    )
```

profile of v0, /device:TPU:0, one launch (start us, length us, event | category | flops | bytes accessed | tf_op | source)
XLA Modules:
  0.0 1140.3 jit_solution(3156177068706588488)
XLA Ops:
  7.2 1.6 convert_element_type.141
  9.0 1.9 convert_element_type.151
  10.9 26.2 %all-gather.20.cloned.1.call-done = bf16[1,768,768]{2,1,0:T(8,128)(2,1)} async-done(((bf16[1,96,768]{2,1,0:T(8,128)(2,1)}), bf16[1,768,768]{2,1,0:T(8,128)(2,1)}) %all-gather.20.cloned.1.call-update) | async-done | bytes 1179664 | tf_op jit(solution)/shard_map/all_gather | solution.py:267
  37.2 31.3 %all-gather.24.cloned.1.call-done = bf16[2,768,768]{2,1,0:T(8,128)(2,1)} async-done(((bf16[2,96,768]{2,1,0:T(8,128)(2,1)}), bf16[2,768,768]{2,1,0:T(8,128)(2,1)}) %all-gather.24.cloned.1.call-update) | async-done | bytes 2359312 | tf_op jit(solution)/shard_map/all_gather | solution.py:268
  70.1 89.4 %all-gather.22.cloned.1.call-done = bf16[4,768,768]{2,1,0:T(8,128)(2,1)} async-done(((bf16[1,768,768]{2,1,0:T(8,128)(2,1)}), bf16[4,768,768]{2,1,0:T(8,128)(2,1)}) %all-gather.22.cloned.1.call-update) | async-done | bytes 4718608 | tf_op jit(solution)/shard_map/all_gather | solution.py:271
  161.3 1.6 fusion.23
  163.1 1.6 convolution_convert_fusion.3
  165.6 1.9 fusion.96
  167.8 158.3 %all-gather.26.cloned.1.call-done = bf16[2,768,3072]{2,1,0:T(8,128)(2,1)} async-done(((bf16[2,768,768]{2,1,0:T(8,128)(2,1)}), bf16[2,768,3072]{2,1,0:T(8,128)(2,1)}) %all-gather.26.cloned.1.call-update) | async-done | bytes 9437200 | tf_op jit(solution)/shard_map/all_gather | solution.py:272
  326.1 4.6 maximum_convert_fusion
  331.4 5.2 fusion.91
  336.7 31.7 %all_gather.83 = bf16[512,768]{1,0:T(8,128)(2,1)} all-gather(bf16[128,768]{1,0:T(8,128)(2,1)S(1)} %add_convert_fusion.1), channel_id=1, replica_groups=mesh['dp'=8,'group'=4] {'group'}, dimensions={0}, use_global_device_ids=true | all-gather | bytes 983040 | tf_op jit(solution)/shard_map/all_gather | solution.py:174
  368.5 30.0 %all_gather.82 = bf16[512,768]{1,0:T(8,128)(2,1)} all-gather(bf16[128,768]{1,0:T(8,128)(2,1)S(1)} %copy.71), channel_id=1, replica_groups=mesh['dp'=8,'group'=4] {'group'}, dimensions={0}, use_global_device_ids=true | all-gather | bytes 983040 | tf_op jit(solution)/shard_map/all_gather | solution.py:175
  398.5 5.0 multiply_reduce_fusion.2
  405.6 1.8 convolution_convert_fusion.1
  413.3 18.2 %all_gather.87 = bf16[512,768]{1,0:T(8,128)(2,1)S(1)} all-gather(bf16[128,768]{1,0:T(8,128)(2,1)} %copy-done.31), channel_id=1, replica_groups=mesh['dp'=8,'group'=4] {'group'}, dimensions={0}, use_global_device_ids=true | all-gather | bytes 983040 | tf_op jit(solution)/shard_map/all_gather | solution.py:179
  431.6 29.5 %all_gather.84 = bf16[512,768]{1,0:T(8,128)(2,1)S(1)} all-gather(bf16[128,768]{1,0:T(8,128)(2,1)S(1)} %copy-done.25), channel_id=1, replica_groups=mesh['dp'=8,'group'=4] {'group'}, dimensions={0}, use_global_device_ids=true | all-gather | bytes 983040 | tf_op jit(solution)/shard_map/all_gather | solution.py:176
  461.1 29.8 %all_gather.85 = bf16[512,768]{1,0:T(8,128)(2,1)S(1)} all-gather(bf16[128,768]{1,0:T(8,128)(2,1)} %copy.73), channel_id=1, replica_groups=mesh['dp'=8,'group'=4] {'group'}, dimensions={0}, use_global_device_ids=true | all-gather | bytes 983040 | tf_op jit(solution)/shard_map/all_gather | solution.py:177
  491.0 28.4 %all_gather.86 = bf16[512,768]{1,0:T(8,128)(2,1)S(1)} all-gather(bf16[128,768]{1,0:T(8,128)(2,1)S(1)} %copy-done.26), channel_id=1, replica_groups=mesh['dp'=8,'group'=4] {'group'}, dimensions={0}, use_global_device_ids=true | all-gather | bytes 983040 | tf_op jit(solution)/shard_map/all_gather | solution.py:178
  519.4 2.5 fusion.42
  522.8 17.2 %all_gather.91 = bf16[512,768]{1,0:T(8,128)(2,1)} all-gather(bf16[128,768]{1,0:T(8,128)(2,1)S(1)} %copy-done.30), channel_id=1, replica_groups=mesh['dp'=8,'group'=4] {'group'}, dimensions={0}, use_global_device_ids=true | all-gather | bytes 983040 | tf_op jit(solution)/shard_map/all_gather | solution.py:181
  540.0 16.6 %all_gather.88 = bf16[512,768]{1,0:T(8,128)(2,1)} all-gather(bf16[128,768]{1,0:T(8,128)(2,1)S(1)} %copy-done.28), channel_id=1, replica_groups=mesh['dp'=8,'group'=4] {'group'}, dimensions={0}, use_global_device_ids=true | all-gather | bytes 983040 | tf_op jit(solution)/shard_map/all_gather | solution.py:180
  556.6 2.3 convolution_bitcast_fusion
  558.9 2.2 convolution_bitcast_fusion.1
  561.1 2.4 pad_maximum_fusion
  564.5 1.8 fusion.37
  566.4 1.8 convolution_add_fusion.4
  568.3 3.2 multiply_reduce_fusion.3
  571.8 2.4 multiply_reduce_fusion.10
  574.9 46.3 %reduce-scatter.5.cloned.1.call-done = f32[2,96,768]{2,1,0:T(8,128)} async-done(((f32[2,768,768]{2,1,0:T(8,128)}), f32[2,96,768]{2,1,0:T(8,128)}) %reduce-scatter.5.cloned.1.call-update) | async-done | bytes 589840 | tf_op jit(solution)/shard_map/reduce_scatter | solution.py:280
  621.2 2.0 multiply_reduce_fusion.1
  623.3 40.2 %all-reduce = (f32[12,768]{1,0:T(8,128)}, f32[6]{0:T(128)S(1)}) all-reduce(f32[12,768]{1,0:T(8,128)S(1)} %concatenate.6, f32[6]{0:T(128)S(1)} %pad_maximum_fusion.1), channel_id=1, replica_groups=mesh['dp'=8,'group'=4] {'dp','group'}, use_global_device_ids=true, to_apply=%region_24.25 | all-reduce | flops 9222 | bytes 73776 | tf_op jit(solution)/shard_map/psum | solution.py:294
  664.5 29.7 %all-gather.42.cloned.1.call-done = bf16[2,768,768]{2,1,0:T(8,128)(2,1)} async-done(((bf16[2,96,768]{2,1,0:T(8,128)(2,1)}), bf16[2,768,768]{2,1,0:T(8,128)(2,1)}) %all-gather.42.cloned.1.call-update) | async-done | bytes 2359312 | tf_op jit(solution)/shard_map/all_gather | solution.py:220
  694.2 3.6 fusion.110
  697.8 39.8 %all-reduce.5.cloned.1.call-done = f32[2,96,768]{2,1,0:T(8,128)} async-done(((f32[2,96,768]{2,1,0:T(8,128)}), f32[2,96,768]{2,1,0:T(8,128)}) %all-reduce.5.cloned.1.call-update) | async-done | bytes 589840 | tf_op jit(solution)/shard_map/psum | solution.py:228
  737.6 1.8 convert_element_type.176
  740.8 1.6 fusion.68
  742.5 26.0 %all-gather.44.cloned.1.call-done = bf16[2,768,768]{2,1,0:T(8,128)(2,1)} async-done(((bf16[2,96,768]{2,1,0:T(8,128)(2,1)}), bf16[2,768,768]{2,1,0:T(8,128)(2,1)}) %all-gather.44.cloned.1.call-update) | async-done | bytes 2359312 | tf_op jit(solution)/shard_map/all_gather | solution.py:233
  768.5 4.0 fusion.102
  772.5 22.2 %all-gather.54.cloned.1.call-done = bf16[1,768,768]{2,1,0:T(8,128)(2,1)} async-done(((bf16[1,96,768]{2,1,0:T(8,128)(2,1)}), bf16[1,768,768]{2,1,0:T(8,128)(2,1)}) %all-gather.54.cloned.1.call-update) | async-done | bytes 1179664 | tf_op jit(solution)/shard_map/all_gather | solution.py:219
  794.7 2.5 fusion.97
  797.3 28.8 %all-gather.46.cloned.1.call-done = bf16[2,768,768]{2,1,0:T(8,128)(2,1)} async-done(((bf16[2,96,768]{2,1,0:T(8,128)(2,1)}), bf16[2,768,768]{2,1,0:T(8,128)(2,1)}) %all-gather.46.cloned.1.call-update) | async-done | bytes 2359312 | tf_op jit(solution)/shard_map/all_gather | solution.py:220
  826.1 3.3 fusion.111
  829.5 22.3 %all-gather.32.cloned.1.call-done = bf16[768,768]{1,0:T(8,128)(2,1)} async-done(((bf16[96,768]{1,0:T(8,128)(2,1)}), bf16[768,768]{1,0:T(8,128)(2,1)}) %all-gather.32.cloned.1.call-update) | async-done | bytes 1179664 | tf_op jit(solution)/shard_map/all_gather | solution.py:232
  851.8 2.6 fusion.98
  854.5 39.2 %all-reduce.7.cloned.1.call-done = f32[2,96,768]{2,1,0:T(8,128)} async-done(((f32[2,96,768]{2,1,0:T(8,128)}), f32[2,96,768]{2,1,0:T(8,128)}) %all-reduce.7.cloned.1.call-update) | async-done | bytes 589840 | tf_op jit(solution)/shard_map/psum | solution.py:228
  893.7 1.8 convert_element_type.179
  895.5 23.3 %all-gather.34.cloned.1.call-done = bf16[768,768]{1,0:T(8,128)(2,1)} async-done(((bf16[96,768]{1,0:T(8,128)(2,1)}), bf16[768,768]{1,0:T(8,128)(2,1)}) %all-gather.34.cloned.1.call-update) | async-done | bytes 1179664 | tf_op jit(solution)/shard_map/all_gather | solution.py:219
  918.8 2.6 fusion.99
  921.5 28.0 %all-gather.48.cloned.1.call-done = bf16[2,768,768]{2,1,0:T(8,128)(2,1)} async-done(((bf16[2,96,768]{2,1,0:T(8,128)(2,1)}), bf16[2,768,768]{2,1,0:T(8,128)(2,1)}) %all-gather.48.cloned.1.call-update) | async-done | bytes 2359312 | tf_op jit(solution)/shard_map/all_gather | solution.py:233
  949.5 3.9 fusion.103
  953.5 21.7 %all-gather.36.cloned.1.call-done = bf16[768,768]{1,0:T(8,128)(2,1)} async-done(((bf16[96,768]{1,0:T(8,128)(2,1)}), bf16[768,768]{1,0:T(8,128)(2,1)}) %all-gather.36.cloned.1.call-update) | async-done | bytes 1179664 | tf_op jit(solution)/shard_map/all_gather | solution.py:232
  975.2 3.2 fusion.100
  978.4 27.6 %all-gather.50.cloned.1.call-done = bf16[2,768,768]{2,1,0:T(8,128)(2,1)} async-done(((bf16[2,96,768]{2,1,0:T(8,128)(2,1)}), bf16[2,768,768]{2,1,0:T(8,128)(2,1)}) %all-gather.50.cloned.1.call-update) | async-done | bytes 2359312 | tf_op jit(solution)/shard_map/all_gather | solution.py:220
  1006.0 3.3 fusion.112
  1009.5 22.2 %all-gather.38.cloned.1.call-done = bf16[768,768]{1,0:T(8,128)(2,1)} async-done(((bf16[96,768]{1,0:T(8,128)(2,1)}), bf16[768,768]{1,0:T(8,128)(2,1)}) %all-gather.38.cloned.1.call-update) | async-done | bytes 1179664 | tf_op jit(solution)/shard_map/all_gather | solution.py:219
  1031.7 2.5 fusion.101
  1034.5 39.2 %all-reduce.9.cloned.1.call-done = f32[2,96,768]{2,1,0:T(8,128)} async-done(((f32[2,96,768]{2,1,0:T(8,128)}), f32[2,96,768]{2,1,0:T(8,128)}) %all-reduce.9.cloned.1.call-update) | async-done | bytes 589840 | tf_op jit(solution)/shard_map/psum | solution.py:228
  1073.7 1.8 convert_element_type.182
  1076.6 4.8 fusion.18
  1082.9 16.1 %all-gather.40.cloned.1.call-done = bf16[768,768]{1,0:T(8,128)(2,1)} async-done(((bf16[96,768]{1,0:T(8,128)(2,1)}), bf16[768,768]{1,0:T(8,128)(2,1)}) %all-gather.40.cloned.1.call-update) | async-done | bytes 1179664 | tf_op jit(solution)/shard_map/all_gather | solution.py:232
  1099.0 3.2 fusion.33
  1102.2 27.6 %all-gather.52.cloned.1.call-done = bf16[2,768,768]{2,1,0:T(8,128)(2,1)} async-done(((bf16[2,96,768]{2,1,0:T(8,128)(2,1)}), bf16[2,768,768]{2,1,0:T(8,128)(2,1)}) %all-gather.52.cloned.1.call-update) | async-done | bytes 2359312 | tf_op jit(solution)/shard_map/all_gather | solution.py:233
  1129.9 3.9 fusion.7
  (228 shorter events, 21.7 us)
Async XLA Ops:
  7.2 29.9 %all-gather.20.cloned.1.call-start = ((), (), s32[]{:S(2)}) async-start(), calls=%async_computation.2 | async-start | bytes 1327104 | tf_op jit(solution)/shard_map/all_gather | solution.py:267
  8.9 59.7 %slice-start = ((f32[12,768]{1,0:T(8,128)}), f32[4,768]{1,0:T(4,128)S(1)}, s32[]{:S(2)}) async-start(f32[12,768]{1,0:T(8,128)} %param.16), calls=%async_computation.25 | async-start | bytes 24576 | tf_op jit(solution)/shard_map/slice | solution.py:45
  8.9 59.7 %copy-start = (f32[128,768]{1,0:T(8,128)S(1)}, f32[128,768]{1,0:T(8,128)}, u32[]{:S(2)}) copy-start(f32[128,768]{1,0:T(8,128)} %param.9) | copy-start | bytes 1179652
  8.9 59.6 %all-gather.24.cloned.1.call-start = ((), (), s32[]{:S(2)}) async-start(), calls=%async_computation.4 | async-start | bytes 2654208 | tf_op jit(solution)/shard_map/all_gather | solution.py:268
  10.8 57.9 %copy-start.55 = (s32[1,4]{1,0:T(1,128)S(1)}, s32[1,4]{1,0:T(1,128)}, u32[]{:S(2)}) copy-start(s32[1,4]{1,0:T(1,128)} %param.11) | copy-start | bytes 52
  10.8 58.2 %copy-start.36 = (f32[12,768]{1,0:T(8,128)S(1)}, f32[12,768]{1,0:T(8,128)}, u32[]{:S(2)}) copy-start(f32[12,768]{1,0:T(8,128)} %param.16) | copy-start | bytes 110596
  10.8 148.7 %all-gather.22.cloned.1.call-start = ((), (), s32[]{:S(2)}) async-start(), calls=%async_computation.3 | async-start | bytes 5898240 | tf_op jit(solution)/shard_map/all_gather | solution.py:271
  37.1 289.0 %all-gather.26.cloned.1.call-start = ((), (), s32[]{:S(2)}) async-start(), calls=%async_computation.5 | async-start | bytes 11796480 | tf_op jit(solution)/shard_map/all_gather | solution.py:272
  68.5 488.0 %all-gather.30.cloned.1.call-start = ((), (), s32[]{:S(2)}) async-start(), calls=%async_computation.8 | async-start | bytes 3932160 | tf_op jit(solution)/shard_map/all_gather | solution.py:183
  69.6 93.2 %copy-start.45 = (f32[128]{0:T(128)}, f32[128]{0:T(128)S(1)}, u32[]{:S(2)}) copy-start(f32[128]{0:T(128)S(1)} %broadcast_multiply_fusion.7) | copy-start | bytes 1540
  69.8 89.7 %copy-start.51 = (f32[128]{0:T(128)}, f32[128]{0:T(128)S(1)}, u32[]{:S(2)}) copy-start(f32[128]{0:T(128)S(1)} %add_rsqrt_fusion.1) | copy-start | bytes 1540
  167.4 231.0 %copy-start.47 = (f32[128]{0:T(128)}, f32[128]{0:T(128)S(1)}, u32[]{:S(2)}) copy-start(f32[128]{0:T(128)S(1)} %broadcast_multiply_fusion.6) | copy-start | bytes 1540
  167.7 230.8 %copy-start.54 = (f32[128]{0:T(128)}, f32[128]{0:T(128)S(1)}, u32[]{:S(2)}) copy-start(f32[128]{0:T(128)S(1)} %add_rsqrt_fusion) | copy-start | bytes 1540
  167.8 162.9 %copy-start.27 = (bf16[128,768]{1,0:T(8,128)(2,1)}, bf16[128,768]{1,0:T(8,128)(2,1)S(1)}, u32[]{:S(2)}) copy-start(bf16[128,768]{1,0:T(8,128)(2,1)S(1)} %add_convert_fusion) | copy-start | bytes 589828
  167.8 163.0 %copy-start.16 = (f32[128,768]{1,0:T(8,128)S(1)}, f32[128,768]{1,0:T(8,128)}, u32[]{:S(2)}) copy-start(f32[128,768]{1,0:T(8,128)} %param.10) | copy-start | bytes 1179652
  330.7 228.2 %all-gather.28.cloned.1.call-start = ((), (), s32[]{:S(2)}) async-start(), calls=%async_computation.7 | async-start | bytes 3932160 | tf_op jit(solution)/shard_map/all_gather | solution.py:182
  336.6 235.2 %reduce-scatter.3.cloned.1.call-start = ((), (), s32[]{:S(2)}) async-start(), calls=%async_computation.6 | async-start | bytes 2654208 | tf_op jit(solution)/shard_map/reduce_scatter | solution.py:279
  409.4 51.7 %copy-start.10 = (bf16[128,12,64]{0,2,1:T(8,128)(2,1)}, bf16[128,12,64]{0,2,1:T(8,128)(2,1)S(1)}, u32[]{:S(2)}) copy-start(bf16[128,12,64]{0,2,1:T(8,128)(2,1)S(1)} %get-tuple-element.47) | copy-start | bytes 589828
  410.6 80.4 %copy-start.12 = (bf16[12,64,128]{2,1,0:T(8,128)(2,1)}, bf16[12,64,128]{2,1,0:T(8,128)(2,1)S(1)}, u32[]{:S(2)}) copy-start(bf16[12,64,128]{2,1,0:T(8,128)(2,1)S(1)} %convolution_convert_fusion) | copy-start | bytes 589828
  410.6 21.0 %copy-start.25 = (bf16[128,768]{1,0:T(8,128)(2,1)S(1)}, bf16[128,768]{1,0:T(8,128)(2,1)}, u32[]{:S(2)}) copy-start(bf16[128,768]{1,0:T(8,128)(2,1)} %copy.72) | copy-start | bytes 589828
  412.5 109.4 %copy-start.20 = (bf16[128,12,64]{0,2,1:T(8,128)(2,1)}, bf16[128,12,64]{0,2,1:T(8,128)(2,1)S(1)}, u32[]{:S(2)}) copy-start(bf16[128,12,64]{0,2,1:T(8,128)(2,1)S(1)} %get-tuple-element.45) | copy-start | bytes 589828
  412.5 106.9 %copy-start.23 = (bf16[512,768]{1,0:T(8,128)(2,1)S(1)}, bf16[512,768]{1,0:T(8,128)(2,1)}, u32[]{:S(2)}) copy-start(bf16[512,768]{1,0:T(8,128)(2,1)} %all_gather.83) | copy-start | bytes 2359300
  412.5 106.9 %copy-start.24 = (bf16[512,768]{1,0:T(8,128)(2,1)S(1)}, bf16[512,768]{1,0:T(8,128)(2,1)}, u32[]{:S(2)}) copy-start(bf16[512,768]{1,0:T(8,128)(2,1)} %all_gather.82) | copy-start | bytes 2359300
  413.3 77.6 %copy-start.26 = (bf16[128,768]{1,0:T(8,128)(2,1)S(1)}, bf16[128,768]{1,0:T(8,128)(2,1)}, u32[]{:S(2)}) copy-start(bf16[128,768]{1,0:T(8,128)(2,1)} %copy.74) | copy-start | bytes 589828
  521.9 18.1 %copy-start.28 = (bf16[128,768]{1,0:T(8,128)(2,1)S(1)}, bf16[128,768]{1,0:T(8,128)(2,1)}, u32[]{:S(2)}) copy-start(bf16[128,768]{1,0:T(8,128)(2,1)} %copy-done.27) | copy-start | bytes 589828
  521.9 99.3 %reduce-scatter.5.cloned.1.call-start = ((), (), s32[]{:S(2)}) async-start(), calls=%async_computation.9 | async-start | bytes 5308416 | tf_op jit(solution)/shard_map/reduce_scatter | solution.py:280
  563.6 130.6 %all-gather.42.cloned.1.call-start = ((), (), s32[]{:S(2)}) async-start(), calls=%async_computation.15 | async-start | bytes 2654208 | tf_op jit(solution)/shard_map/all_gather | solution.py:220
  566.4 5.4 copy-start.34
  568.3 53.0 %copy-start.32 = (f32[2,96,768]{2,1,0:T(8,128)S(1)}, f32[2,96,768]{2,1,0:T(8,128)}, u32[]{:S(2)}) copy-start(f32[2,96,768]{2,1,0:T(8,128)} %param.15) | copy-start | bytes 1769476
  623.2 41.3 %copy-start.4 = (f32[2,96,768]{2,1,0:T(8,128)}, f32[2,96,768]{2,1,0:T(8,128)S(1)}, u32[]{:S(2)}) copy-start(f32[2,96,768]{2,1,0:T(8,128)S(1)} %get-tuple-element.36) | copy-start | bytes 1769476
  664.4 73.1 %all-reduce.5.cloned.1.call-start = ((), (), s32[]{:S(2)}) async-start(), calls=%async_computation.16 | async-start | bytes 1179648 | tf_op jit(solution)/shard_map/psum | solution.py:228
  694.2 45.3 %copy-start.57 = (f32[6]{0:T(128)S(1)}, f32[6]{0:T(128)}, u32[]{:S(2)}) copy-start(f32[6]{0:T(128)} %copy-done.56) | copy-start | bytes 76
  694.2 74.3 %copy-start.3 = (bf16[2,768,768]{2,1,0:T(8,128)(2,1)S(1)}, bf16[2,768,768]{2,1,0:T(8,128)(2,1)}, u32[]{:S(2)}) copy-start(bf16[2,768,768]{2,1,0:T(8,128)(2,1)} %all-gather.42.cloned.1.call-done) | copy-start | bytes 7077892
  697.8 70.7 %all-gather.44.cloned.1.call-start = ((), (), s32[]{:S(2)}) async-start(), calls=%async_computation.17 | async-start | bytes 2654208 | tf_op jit(solution)/shard_map/all_gather | solution.py:233
  739.4 55.3 %all-gather.54.cloned.1.call-start = ((), (), s32[]{:S(2)}) async-start(), calls=%async_computation.24 | async-start | bytes 1327104 | tf_op jit(solution)/shard_map/all_gather | solution.py:219
  742.5 83.7 %all-gather.46.cloned.1.call-start = ((), (), s32[]{:S(2)}) async-start(), calls=%async_computation.18 | async-start | bytes 2654208 | tf_op jit(solution)/shard_map/all_gather | solution.py:220
  772.4 53.7 %copy-start.8 = (bf16[2,96,768]{2,1,0:T(8,128)(2,1)S(1)}, bf16[2,96,768]{2,1,0:T(8,128)(2,1)}, u32[]{:S(2)}) copy-start(bf16[2,96,768]{2,1,0:T(8,128)(2,1)} %get-tuple-element.71) | copy-start | bytes 884740
  772.5 79.3 %all-gather.32.cloned.1.call-start = ((), (), s32[]{:S(2)}) async-start(), calls=%async_computation.10 | async-start | bytes 1327104 | tf_op jit(solution)/shard_map/all_gather | solution.py:232
  797.3 54.5 %copy-start.5 = (bf16[1,768,768]{2,1,0:T(8,128)(2,1)S(1)}, bf16[1,768,768]{2,1,0:T(8,128)(2,1)}, u32[]{:S(2)}) copy-start(bf16[1,768,768]{2,1,0:T(8,128)(2,1)} %all-gather.54.cloned.1.call-done) | copy-start | bytes 3538948
  797.3 54.5 %copy-start.7 = (f32[1,96,768]{2,1,0:T(8,128)S(1)}, f32[1,96,768]{2,1,0:T(8,128)}, u32[]{:S(2)}) copy-start(f32[1,96,768]{2,1,0:T(8,128)} %get-tuple-element.33) | copy-start | bytes 884740
  797.3 54.5 %copy-start.19 = (bf16[96,768]{1,0:T(8,128)(2,1)S(1)}, bf16[96,768]{1,0:T(8,128)(2,1)}, u32[]{:S(2)}) copy-start(bf16[96,768]{1,0:T(8,128)(2,1)} %get-tuple-element.61) | copy-start | bytes 442372
  797.3 96.4 %all-reduce.7.cloned.1.call-start = ((), (), s32[]{:S(2)}) async-start(), calls=%async_computation.19 | async-start | bytes 1179648 | tf_op jit(solution)/shard_map/psum | solution.py:228
  829.4 89.4 %all-gather.34.cloned.1.call-start = ((), (), s32[]{:S(2)}) async-start(), calls=%async_computation.11 | async-start | bytes 1327104 | tf_op jit(solution)/shard_map/all_gather | solution.py:219
  854.4 95.1 %copy-start.2 = (bf16[2,768,768]{2,1,0:T(8,128)(2,1)S(1)}, bf16[2,768,768]{2,1,0:T(8,128)(2,1)}, u32[]{:S(2)}) copy-start(bf16[2,768,768]{2,1,0:T(8,128)(2,1)} %all-gather.46.cloned.1.call-done) | copy-start | bytes 7077892
  854.5 95.0 %all-gather.48.cloned.1.call-start = ((), (), s32[]{:S(2)}) async-start(), calls=%async_computation.20 | async-start | bytes 2654208 | tf_op jit(solution)/shard_map/all_gather | solution.py:233
  895.5 79.7 %all-gather.36.cloned.1.call-start = ((), (), s32[]{:S(2)}) async-start(), calls=%async_computation.12 | async-start | bytes 1327104 | tf_op jit(solution)/shard_map/all_gather | solution.py:232
  921.5 84.5 %all-gather.50.cloned.1.call-start = ((), (), s32[]{:S(2)}) async-start(), calls=%async_computation.21 | async-start | bytes 2654208 | tf_op jit(solution)/shard_map/all_gather | solution.py:220
  953.5 52.5 %copy-start.6 = (bf16[2,96,768]{2,1,0:T(8,128)(2,1)S(1)}, bf16[2,96,768]{2,1,0:T(8,128)(2,1)}, u32[]{:S(2)}) copy-start(bf16[2,96,768]{2,1,0:T(8,128)(2,1)} %get-tuple-element.73) | copy-start | bytes 884740
  953.5 78.2 %all-gather.38.cloned.1.call-start = ((), (), s32[]{:S(2)}) async-start(), calls=%async_computation.13 | async-start | bytes 1327104 | tf_op jit(solution)/shard_map/all_gather | solution.py:219
  978.4 53.3 %copy-start.18 = (bf16[96,768]{1,0:T(8,128)(2,1)S(1)}, bf16[96,768]{1,0:T(8,128)(2,1)}, u32[]{:S(2)}) copy-start(bf16[96,768]{1,0:T(8,128)(2,1)} %get-tuple-element.67) | copy-start | bytes 442372
  978.4 95.3 %all-reduce.9.cloned.1.call-start = ((), (), s32[]{:S(2)}) async-start(), calls=%async_computation.22 | async-start | bytes 1179648 | tf_op jit(solution)/shard_map/psum | solution.py:228
  1009.4 66.2 %copy-start.59 = (f32[128]{0:T(128)S(1)}, f32[128]{0:T(128)}, u32[]{:S(2)}) copy-start(f32[128]{0:T(128)} %get-tuple-element.14) | copy-start | bytes 1540
  1009.4 66.2 %copy-start.58 = (f32[128]{0:T(128)S(1)}, f32[128]{0:T(128)}, u32[]{:S(2)}) copy-start(f32[128]{0:T(128)} %get-tuple-element.15) | copy-start | bytes 1540
  1009.4 66.3 %copy-start.33 = (f32[128,768]{1,0:T(8,128)S(1)}, f32[128,768]{1,0:T(8,128)}, u32[]{:S(2)}) copy-start(f32[128,768]{1,0:T(8,128)} %get-tuple-element.60) | copy-start | bytes 1179652
  1009.4 66.3 %copy-start.53 = (f32[128]{0:T(128)S(1)}, f32[128]{0:T(128)}, u32[]{:S(2)}) copy-start(f32[128]{0:T(128)} %copy-done.51) | copy-start | bytes 1540
  1009.4 67.2 %copy-start.22 = (bf16[128,3072]{1,0:T(8,128)(2,1)S(1)}, bf16[128,3072]{1,0:T(8,128)(2,1)}, u32[]{:S(2)}) copy-start(bf16[128,3072]{1,0:T(8,128)(2,1)} %get-tuple-element.52) | copy-start | bytes 2359300
  1009.4 67.2 %copy-start.48 = (f32[768]{0:T(1024)S(1)}, f32[768]{0:T(1024)}, u32[]{:S(2)}) copy-start(f32[768]{0:T(1024)} %get-tuple-element.19) | copy-start | bytes 9220
  1009.4 89.6 %all-gather.40.cloned.1.call-start = ((), (), s32[]{:S(2)}) async-start(), calls=%async_computation.14 | async-start | bytes 1327104 | tf_op jit(solution)/shard_map/all_gather | solution.py:232
  1034.2 95.6 %all-gather.52.cloned.1.call-start = ((), (), s32[]{:S(2)}) async-start(), calls=%async_computation.23 | async-start | bytes 2654208 | tf_op jit(solution)/shard_map/all_gather | solution.py:233
  1076.6 5.6 copy-start.37
  1076.6 22.5 %copy-start.17 = (bf16[96,768]{1,0:T(8,128)(2,1)S(1)}, bf16[96,768]{1,0:T(8,128)(2,1)}, u32[]{:S(2)}) copy-start(bf16[96,768]{1,0:T(8,128)(2,1)} %get-tuple-element.69) | copy-start | bytes 442372
  1081.4 48.4 %copy-start.1 = (bf16[2,768,768]{2,1,0:T(8,128)(2,1)S(1)}, bf16[2,768,768]{2,1,0:T(8,128)(2,1)}, u32[]{:S(2)}) copy-start(bf16[2,768,768]{2,1,0:T(8,128)(2,1)} %all-gather.50.cloned.1.call-done) | copy-start | bytes 7077892
  1081.4 48.4 %copy-start.9 = (f32[2,96,768]{2,1,0:T(8,128)S(1)}, f32[2,96,768]{2,1,0:T(8,128)}, u32[]{:S(2)}) copy-start(f32[2,96,768]{2,1,0:T(8,128)} %get-tuple-element.74) | copy-start | bytes 1769476
  1082.2 51.6 %copy-start.35 = (f32[12,768]{1,0:T(8,128)}, f32[12,768]{1,0:T(8,128)S(1)}, u32[]{:S(2)}) copy-start(f32[12,768]{1,0:T(8,128)S(1)} %get-tuple-element.30) | copy-start | bytes 110596
  (20 other events, 71.1 us)
Sparse Core Ops, SparseCore 0:
  10.4 26.6 all-gather.19
  39.6 28.8 all-gather.23
  70.1 89.3 all-gather.21
  160.9 165.1 all-gather.25
  330.8 85.3 all-gather.29
  417.6 102.2 all-gather.27
  523.3 40.7 reduce-scatter.2
  567.5 53.7 reduce-scatter.4
  664.6 29.5 all-gather.41
  697.9 39.6 all-reduce.4
  740.1 28.3 all-gather.43
  770.8 23.9 all-gather.53
  797.2 28.8 all-gather.45
  827.8 23.9 all-gather.31
  854.0 39.6 all-reduce.6
  895.4 23.3 all-gather.33
  920.6 28.8 all-gather.47
  951.2 23.9 all-gather.35
  977.1 28.8 all-gather.49
  1007.7 23.9 all-gather.37
  1034.0 39.6 all-reduce.8
  1075.6 23.3 all-gather.39
  1100.9 28.8 all-gather.51
where the time goes:
time: 1140 us
  waiting for transfers between devices  766 us (67%)
  blocking collectives  242 us (21%)
  matrix products  83.9 us (7%)
  other arithmetic  25.5 us (2%)
  between operations  15.5 us (1%)
    all_gather x1, waiting for transfers between devices, on_device(): lax.all_gather(ffn_rows, 'group', axis=2, tiled=True)  158 us
    psum x3, waiting for transfers between devices, orthogonalize_rows(): ffn_gram = lax.psum(ffn_part, 'group')  118 us
    all_gather x1, waiting for transfers between devices, on_device(): lax.all_gather(attn_rows, 'group', axis=0, tiled=True)  89.4 us
    all_gather x3, waiting for transfers between devices, orthogonalize_rows(): lax.all_gather(ffn_iter_b, 'dp', axis=1, tiled=True)  86 us
    all_gather x3, waiting for transfers between devices, orthogonalize_rows(): lax.all_gather(ffn_gram_b, 'dp', axis=1, tiled=True)  81.6 us
    all_gather x3, waiting for transfers between devices, orthogonalize_rows(): lax.all_gather(attn_iter_b, 'dp', axis=0, tiled=True)  67.7 us
    all_gather x3, waiting for transfers between devices, orthogonalize_rows(): lax.all_gather(attn_gram_b, 'dp', axis=0, tiled=True)  60.1 us
    reduce_scatter x1, waiting for transfers between devices, on_device(): lax.psum_scatter(ffn_term, 'dp', scatter_dimension=1, tiled=True)  46.3 us
  transfers between devices with their start and end apart: 23, of which 20 were waited for; matrix products, arithmetic and copies ran while one was open for 8% of the time, Pallas kernels for 0%

commit v1 on v0

--- a/solution.py
+++ b/solution.py
@@ -12,6 +12,19 @@
 momentum_rate = 0.9
 muon_rate = 0.8
 vector_rate = 0.1
+
+
+def ring_gather(x, axis, dim):
+    size, index, span = (lax.axis_size(axis), lax.axis_index(axis), x.shape[dim])
+    right = [(i, (i + 1) % size) for i in range(size)]
+    out = jnp.zeros((*x.shape[:dim], size * span, *x.shape[dim + 1 :]), x.dtype)
+    block = x
+    for turn in range(size):
+        owner = (index - turn) % size
+        out = lax.dynamic_update_slice_in_dim(out, block, owner * span, axis=dim)
+        if turn < size - 1:
+            block = lax.ppermute(block, axis, right)
+    return out
 
 
 def norm_forward(rows):
@@ -268,7 +281,7 @@
         lax.all_gather(own_ffn, "dp", axis=1, tiled=True),
     )
     attn_whole, ffn_whole = (
-        lax.all_gather(attn_rows, "group", axis=0, tiled=True),
+        ring_gather(attn_rows, "group", 0),
         lax.all_gather(ffn_rows, "group", axis=2, tiled=True),
     )
     outputs, input_grad, vector_terms, pieces = layer_block(

time: 1140 us -> 1120 us (0.982)
  waiting for transfers between devices: 766 us -> 692 us
  starting transfers between devices: 1.17 us -> 50.5 us
    ppermute x0 -> x3, waiting for transfers between devices: none -> 141 us  [ring_gather(): block = lax.ppermute(block, axis, right)]
    all_gather x1, waiting for transfers between devices: 158 us -> 30.1 us  [on_device(): lax.all_gather(ffn_rows, 'group', axis=2, tiled=True)]
    all_gather x1 -> x0, waiting for transfers between devices: 89.4 us -> none  [on_device(): lax.all_gather(attn_rows, 'group', axis=0, tiled=True)]
    ppermute x0 -> x3, starting transfers between devices: none -> 49.3 us  [ring_gather(): block = lax.ppermute(block, axis, right)]
  transfers between devices with their start and end apart: 23 -> 25, of which waited for: 20 -> 22; matrix products, arithmetic and copies ran while one was open for 8% -> 8% of each run, Pallas kernels for 0% -> 0%
where the time goes in v1:
time: 1120 us
  waiting for transfers between devices  692 us (62%)
  blocking collectives  243 us (22%)
  matrix products  82.5 us (7%)
  starting transfers between devices  50.5 us (5%)
  other arithmetic  25.5 us (2%)
  between operations  15.8 us (1%)
    ppermute x3, waiting for transfers between devices, ring_gather(): block = lax.ppermute(block, axis, right)  141 us
    psum x3, waiting for transfers between devices, orthogonalize_rows(): ffn_gram = lax.psum(ffn_part, 'group')  118 us
    all_gather x3, waiting for transfers between devices, orthogonalize_rows(): lax.all_gather(ffn_iter_b, 'dp', axis=1, tiled=True)  85.7 us
    all_gather x3, waiting for transfers between devices, orthogonalize_rows(): lax.all_gather(ffn_gram_b, 'dp', axis=1, tiled=True)  81.4 us
    all_gather x3, waiting for transfers between devices, orthogonalize_rows(): lax.all_gather(attn_iter_b, 'dp', axis=0, tiled=True)  68 us
    all_gather x3, waiting for transfers between devices, orthogonalize_rows(): lax.all_gather(attn_gram_b, 'dp', axis=0, tiled=True)  60.2 us
    ppermute x3, starting transfers between devices, ring_gather(): block = lax.ppermute(block, axis, right)  49.3 us
    reduce_scatter x1, waiting for transfers between devices, on_device(): lax.psum_scatter(ffn_term, 'dp', scatter_dimension=1, tiled=True)  48.9 us
  transfers between devices with their start and end apart: 25, of which 22 were waited for; matrix products, arithmetic and copies ran while one was open for 8% of the time, Pallas kernels for 0%

profile of v1, /device:TPU:0, one launch (start us, length us, event | category | flops | bytes accessed | tf_op | source)
XLA Modules:
  0.0 1120.3 jit_solution(14885148961381147243)
XLA Ops:
  7.3 1.9 convert_element_type.151
  10.9 31.2 %all-gather.21.cloned.1.call-done = bf16[2,768,768]{2,1,0:T(8,128)(2,1)} async-done(((bf16[2,96,768]{2,1,0:T(8,128)(2,1)}), bf16[2,768,768]{2,1,0:T(8,128)(2,1)}) %all-gather.21.cloned.1.call-update) | async-done | bytes 2359312 | tf_op jit(solution)/shard_map/all_gather | solution.py:281
  42.2 26.3 %all-gather.19.cloned.1.call-done = bf16[1,768,768]{2,1,0:T(8,128)(2,1)} async-done(((bf16[1,96,768]{2,1,0:T(8,128)(2,1)}), bf16[1,768,768]{2,1,0:T(8,128)(2,1)}) %all-gather.19.cloned.1.call-update) | async-done | bytes 1179664 | tf_op jit(solution)/shard_map/all_gather | solution.py:280
  70.0 43.6 %collective-permute-done = bf16[1,768,768]{2,1,0:T(8,128)(2,1)S(1)} collective-permute-done((bf16[1,768,768]{2,1,0:T(8,128)(2,1)}, bf16[1,768,768]{2,1,0:T(8,128)(2,1)S(1)}, u32[]{:S(2)}, u32[]{:S(2)}) %collective-permute-start) | collective-permute-done | bytes 1179680 | tf_op jit(solution)/shard_map/ppermute | solution.py:26
  113.7 18.1 %collective-permute-start.1 = (bf16[1,768,768]{2,1,0:T(8,128)(2,1)S(1)}, bf16[1,768,768]{2,1,0:T(8,128)(2,1)S(1)}, u32[]{:S(2)}, u32[]{:S(2)}) collective-permute-start(bf16[1,768,768]{2,1,0:T(8,128)(2,1)S(1)} %collective-permute-done), channel_id=1, source_target_pairs={{0,1},{1,2},{2,3},{3,0},{4,5},{5,6},{6,7},{7,4},{8,9},{9,10},{10,1... | collective-permute-start | bytes 3538952 | tf_op jit(solution)/shard_map/ppermute | solution.py:26
  132.9 48.5 %collective-permute-done.1 = bf16[1,768,768]{2,1,0:T(8,128)(2,1)S(1)} collective-permute-done((bf16[1,768,768]{2,1,0:T(8,128)(2,1)S(1)}, bf16[1,768,768]{2,1,0:T(8,128)(2,1)S(1)}, u32[]{:S(2)}, u32[]{:S(2)}) %collective-permute-start.1) | collective-permute-done | bytes 1179680 | tf_op jit(solution)/shard_map/ppermute | solution.py:26
  181.4 29.8 %collective-permute-start.2 = (bf16[1,768,768]{2,1,0:T(8,128)(2,1)S(1)}, bf16[1,768,768]{2,1,0:T(8,128)(2,1)S(1)}, u32[]{:S(2)}, u32[]{:S(2)}) collective-permute-start(bf16[1,768,768]{2,1,0:T(8,128)(2,1)S(1)} %collective-permute-done.1), channel_id=1, source_target_pairs={{0,1},{1,2},{2,3},{3,0},{4,5},{5,6},{6,7},{7,4},{8,9},{9,10},{10,1... | collective-permute-start | bytes 3538952 | tf_op jit(solution)/shard_map/ppermute | solution.py:26
  213.1 49.1 %collective-permute-done.2 = bf16[1,768,768]{2,1,0:T(8,128)(2,1)S(1)} collective-permute-done((bf16[1,768,768]{2,1,0:T(8,128)(2,1)S(1)}, bf16[1,768,768]{2,1,0:T(8,128)(2,1)S(1)}, u32[]{:S(2)}, u32[]{:S(2)}) %collective-permute-start.2) | collective-permute-done | bytes 1179680 | tf_op jit(solution)/shard_map/ppermute | solution.py:26
  262.3 2.2 copy-done
  271.4 30.1 %all-gather.23.cloned.1.call-done = bf16[2,768,3072]{2,1,0:T(8,128)(2,1)} async-done(((bf16[2,768,768]{2,1,0:T(8,128)(2,1)}), bf16[2,768,3072]{2,1,0:T(8,128)(2,1)}) %all-gather.23.cloned.1.call-update) | async-done | bytes 9437200 | tf_op jit(solution)/shard_map/all_gather | solution.py:285
  301.5 4.6 maximum_convert_fusion
  306.8 5.2 fusion.93
  312.1 30.6 %all_gather.79 = bf16[512,768]{1,0:T(8,128)(2,1)} all-gather(bf16[128,768]{1,0:T(8,128)(2,1)S(1)} %add_convert_fusion.1), channel_id=1, replica_groups=mesh['dp'=8,'group'=4] {'group'}, dimensions={0}, use_global_device_ids=true | all-gather | bytes 983040 | tf_op jit(solution)/shard_map/all_gather | solution.py:187
  342.9 28.2 %all_gather.78 = bf16[512,768]{1,0:T(8,128)(2,1)} all-gather(bf16[128,768]{1,0:T(8,128)(2,1)S(1)} %copy.58), channel_id=1, replica_groups=mesh['dp'=8,'group'=4] {'group'}, dimensions={0}, use_global_device_ids=true | all-gather | bytes 983040 | tf_op jit(solution)/shard_map/all_gather | solution.py:188
  371.1 5.0 multiply_reduce_fusion.2
  378.3 1.8 convolution_convert_fusion.1
  386.0 21.3 %all_gather.83 = bf16[512,768]{1,0:T(8,128)(2,1)S(1)} all-gather(bf16[128,768]{1,0:T(8,128)(2,1)} %copy-done.34), channel_id=1, replica_groups=mesh['dp'=8,'group'=4] {'group'}, dimensions={0}, use_global_device_ids=true | all-gather | bytes 983040 | tf_op jit(solution)/shard_map/all_gather | solution.py:192
  407.3 28.9 %all_gather.80 = bf16[512,768]{1,0:T(8,128)(2,1)S(1)} all-gather(bf16[128,768]{1,0:T(8,128)(2,1)S(1)} %copy-done.28), channel_id=1, replica_groups=mesh['dp'=8,'group'=4] {'group'}, dimensions={0}, use_global_device_ids=true | all-gather | bytes 983040 | tf_op jit(solution)/shard_map/all_gather | solution.py:189
  436.2 29.1 %all_gather.81 = bf16[512,768]{1,0:T(8,128)(2,1)S(1)} all-gather(bf16[128,768]{1,0:T(8,128)(2,1)} %copy.60), channel_id=1, replica_groups=mesh['dp'=8,'group'=4] {'group'}, dimensions={0}, use_global_device_ids=true | all-gather | bytes 983040 | tf_op jit(solution)/shard_map/all_gather | solution.py:190
  465.3 28.5 %all_gather.82 = bf16[512,768]{1,0:T(8,128)(2,1)S(1)} all-gather(bf16[128,768]{1,0:T(8,128)(2,1)S(1)} %copy-done.29), channel_id=1, replica_groups=mesh['dp'=8,'group'=4] {'group'}, dimensions={0}, use_global_device_ids=true | all-gather | bytes 983040 | tf_op jit(solution)/shard_map/all_gather | solution.py:191
  493.8 2.5 fusion.44
  497.2 19.9 %all_gather.87 = bf16[512,768]{1,0:T(8,128)(2,1)} all-gather(bf16[128,768]{1,0:T(8,128)(2,1)S(1)} %copy-done.33), channel_id=1, replica_groups=mesh['dp'=8,'group'=4] {'group'}, dimensions={0}, use_global_device_ids=true | all-gather | bytes 983040 | tf_op jit(solution)/shard_map/all_gather | solution.py:194
  517.1 16.6 %all_gather.84 = bf16[512,768]{1,0:T(8,128)(2,1)} all-gather(bf16[128,768]{1,0:T(8,128)(2,1)S(1)} %copy-done.31), channel_id=1, replica_groups=mesh['dp'=8,'group'=4] {'group'}, dimensions={0}, use_global_device_ids=true | all-gather | bytes 983040 | tf_op jit(solution)/shard_map/all_gather | solution.py:193
  533.7 2.2 convolution_bitcast_fusion
  536.0 2.2 convolution_bitcast_fusion.1
  538.2 2.4 pad_maximum_fusion
  541.6 1.8 fusion.38
  543.5 1.8 fusion.39
  545.4 3.2 multiply_reduce_fusion.3
  548.9 2.4 multiply_reduce_fusion.10
  552.0 48.9 %reduce-scatter.5.cloned.1.call-done = f32[2,96,768]{2,1,0:T(8,128)} async-done(((f32[2,768,768]{2,1,0:T(8,128)}), f32[2,96,768]{2,1,0:T(8,128)}) %reduce-scatter.5.cloned.1.call-update) | async-done | bytes 589840 | tf_op jit(solution)/shard_map/reduce_scatter | solution.py:293
  600.9 2.0 multiply_reduce_fusion.1
  603.0 40.2 %all-reduce = (f32[12,768]{1,0:T(8,128)}, f32[6]{0:T(128)S(1)}) all-reduce(f32[12,768]{1,0:T(8,128)S(1)} %concatenate.6, f32[6]{0:T(128)S(1)} %pad_maximum_fusion.1), channel_id=1, replica_groups=mesh['dp'=8,'group'=4] {'dp','group'}, use_global_device_ids=true, to_apply=%region_24.25 | all-reduce | flops 9222 | bytes 73776 | tf_op jit(solution)/shard_map/psum | solution.py:307
  644.2 29.7 %all-gather.39.cloned.1.call-done = bf16[2,768,768]{2,1,0:T(8,128)(2,1)} async-done(((bf16[2,96,768]{2,1,0:T(8,128)(2,1)}), bf16[2,768,768]{2,1,0:T(8,128)(2,1)}) %all-gather.39.cloned.1.call-update) | async-done | bytes 2359312 | tf_op jit(solution)/shard_map/all_gather | solution.py:233
  673.9 3.6 fusion.112
  677.5 39.8 %all-reduce.5.cloned.1.call-done = f32[2,96,768]{2,1,0:T(8,128)} async-done(((f32[2,96,768]{2,1,0:T(8,128)}), f32[2,96,768]{2,1,0:T(8,128)}) %all-reduce.5.cloned.1.call-update) | async-done | bytes 589840 | tf_op jit(solution)/shard_map/psum | solution.py:241
  717.2 1.8 convert_element_type.176
  722.2 25.8 %all-gather.41.cloned.1.call-done = bf16[2,768,768]{2,1,0:T(8,128)(2,1)} async-done(((bf16[2,96,768]{2,1,0:T(8,128)(2,1)}), bf16[2,768,768]{2,1,0:T(8,128)(2,1)}) %all-gather.41.cloned.1.call-update) | async-done | bytes 2359312 | tf_op jit(solution)/shard_map/all_gather | solution.py:246
  748.0 4.0 fusion.104
  752.0 22.4 %all-gather.51.cloned.1.call-done = bf16[1,768,768]{2,1,0:T(8,128)(2,1)} async-done(((bf16[1,96,768]{2,1,0:T(8,128)(2,1)}), bf16[1,768,768]{2,1,0:T(8,128)(2,1)}) %all-gather.51.cloned.1.call-update) | async-done | bytes 1179664 | tf_op jit(solution)/shard_map/all_gather | solution.py:232
  774.4 2.5 fusion.99
  777.0 28.6 %all-gather.43.cloned.1.call-done = bf16[2,768,768]{2,1,0:T(8,128)(2,1)} async-done(((bf16[2,96,768]{2,1,0:T(8,128)(2,1)}), bf16[2,768,768]{2,1,0:T(8,128)(2,1)}) %all-gather.43.cloned.1.call-update) | async-done | bytes 2359312 | tf_op jit(solution)/shard_map/all_gather | solution.py:233
  805.6 3.3 fusion.113
  809.0 22.4 %all-gather.29.cloned.1.call-done = bf16[768,768]{1,0:T(8,128)(2,1)} async-done(((bf16[96,768]{1,0:T(8,128)(2,1)}), bf16[768,768]{1,0:T(8,128)(2,1)}) %all-gather.29.cloned.1.call-update) | async-done | bytes 1179664 | tf_op jit(solution)/shard_map/all_gather | solution.py:245
  831.5 2.6 fusion.100
  834.2 39.2 %all-reduce.7.cloned.1.call-done = f32[2,96,768]{2,1,0:T(8,128)} async-done(((f32[2,96,768]{2,1,0:T(8,128)}), f32[2,96,768]{2,1,0:T(8,128)}) %all-reduce.7.cloned.1.call-update) | async-done | bytes 589840 | tf_op jit(solution)/shard_map/psum | solution.py:241
  873.3 1.8 convert_element_type.179
  875.2 23.3 %all-gather.31.cloned.1.call-done = bf16[768,768]{1,0:T(8,128)(2,1)} async-done(((bf16[96,768]{1,0:T(8,128)(2,1)}), bf16[768,768]{1,0:T(8,128)(2,1)}) %all-gather.31.cloned.1.call-update) | async-done | bytes 1179664 | tf_op jit(solution)/shard_map/all_gather | solution.py:232
  898.5 2.6 fusion.101
  901.2 28.0 %all-gather.45.cloned.1.call-done = bf16[2,768,768]{2,1,0:T(8,128)(2,1)} async-done(((bf16[2,96,768]{2,1,0:T(8,128)(2,1)}), bf16[2,768,768]{2,1,0:T(8,128)(2,1)}) %all-gather.45.cloned.1.call-update) | async-done | bytes 2359312 | tf_op jit(solution)/shard_map/all_gather | solution.py:246
  929.2 4.0 fusion.105
  933.3 21.6 %all-gather.33.cloned.1.call-done = bf16[768,768]{1,0:T(8,128)(2,1)} async-done(((bf16[96,768]{1,0:T(8,128)(2,1)}), bf16[768,768]{1,0:T(8,128)(2,1)}) %all-gather.33.cloned.1.call-update) | async-done | bytes 1179664 | tf_op jit(solution)/shard_map/all_gather | solution.py:245
  954.9 3.2 fusion.102
  958.1 27.4 %all-gather.47.cloned.1.call-done = bf16[2,768,768]{2,1,0:T(8,128)(2,1)} async-done(((bf16[2,96,768]{2,1,0:T(8,128)(2,1)}), bf16[2,768,768]{2,1,0:T(8,128)(2,1)}) %all-gather.47.cloned.1.call-update) | async-done | bytes 2359312 | tf_op jit(solution)/shard_map/all_gather | solution.py:233
  985.6 3.3 fusion.114
  989.0 22.4 %all-gather.35.cloned.1.call-done = bf16[768,768]{1,0:T(8,128)(2,1)} async-done(((bf16[96,768]{1,0:T(8,128)(2,1)}), bf16[768,768]{1,0:T(8,128)(2,1)}) %all-gather.35.cloned.1.call-update) | async-done | bytes 1179664 | tf_op jit(solution)/shard_map/all_gather | solution.py:232
  1011.4 2.5 fusion.103
  1014.2 39.0 %all-reduce.9.cloned.1.call-done = f32[2,96,768]{2,1,0:T(8,128)} async-done(((f32[2,96,768]{2,1,0:T(8,128)}), f32[2,96,768]{2,1,0:T(8,128)}) %all-reduce.9.cloned.1.call-update) | async-done | bytes 589840 | tf_op jit(solution)/shard_map/psum | solution.py:241
  1053.3 1.8 convert_element_type.182
  1056.1 4.8 fusion.19
  1062.4 16.2 %all-gather.37.cloned.1.call-done = bf16[768,768]{1,0:T(8,128)(2,1)} async-done(((bf16[96,768]{1,0:T(8,128)(2,1)}), bf16[768,768]{1,0:T(8,128)(2,1)}) %all-gather.37.cloned.1.call-update) | async-done | bytes 1179664 | tf_op jit(solution)/shard_map/all_gather | solution.py:245
  1078.6 3.2 fusion.34
  1081.8 27.6 %all-gather.49.cloned.1.call-done = bf16[2,768,768]{2,1,0:T(8,128)(2,1)} async-done(((bf16[2,96,768]{2,1,0:T(8,128)(2,1)}), bf16[2,768,768]{2,1,0:T(8,128)(2,1)}) %all-gather.49.cloned.1.call-update) | async-done | bytes 2359312 | tf_op jit(solution)/shard_map/all_gather | solution.py:246
  1109.4 4.0 fusion.7
  (240 shorter events, 31.7 us)
Async XLA Ops:
  7.2 124.6 %copy-start.59 = (s32[1,4]{1,0:T(1,128)S(1)}, s32[1,4]{1,0:T(1,128)}, u32[]{:S(2)}) copy-start(s32[1,4]{1,0:T(1,128)} %param.11) | copy-start | bytes 52
  7.2 124.8 %slice-start = ((f32[12,768]{1,0:T(8,128)}), f32[4,768]{1,0:T(4,128)S(1)}, s32[]{:S(2)}) async-start(f32[12,768]{1,0:T(8,128)} %param.16), calls=%async_computation.24 | async-start | bytes 24576 | tf_op jit(solution)/shard_map/slice | solution.py:58
  7.2 124.9 %copy-start.38 = (f32[12,768]{1,0:T(8,128)S(1)}, f32[12,768]{1,0:T(8,128)}, u32[]{:S(2)}) copy-start(f32[12,768]{1,0:T(8,128)} %param.16) | copy-start | bytes 110596
  7.2 124.7 %copy-start.1 = (f32[128,768]{1,0:T(8,128)S(1)}, f32[128,768]{1,0:T(8,128)}, u32[]{:S(2)}) copy-start(f32[128,768]{1,0:T(8,128)} %param.9) | copy-start | bytes 1179652
  7.2 34.9 %all-gather.21.cloned.1.call-start = ((), (), s32[]{:S(2)}) async-start(), calls=%async_computation.3 | async-start | bytes 2654208 | tf_op jit(solution)/shard_map/all_gather | solution.py:281
  9.2 59.4 %all-gather.19.cloned.1.call-start = ((), (), s32[]{:S(2)}) async-start(), calls=%async_computation.2 | async-start | bytes 1327104 | tf_op jit(solution)/shard_map/all_gather | solution.py:280
  10.9 290.7 %all-gather.23.cloned.1.call-start = ((), (), s32[]{:S(2)}) async-start(), calls=%async_computation.4 | async-start | bytes 11796480 | tf_op jit(solution)/shard_map/all_gather | solution.py:285
  42.2 491.6 %all-gather.27.cloned.1.call-start = ((), (), s32[]{:S(2)}) async-start(), calls=%async_computation.7 | async-start | bytes 3932160 | tf_op jit(solution)/shard_map/all_gather | solution.py:196
  68.5 45.1 %collective-permute-start = (bf16[1,768,768]{2,1,0:T(8,128)(2,1)}, bf16[1,768,768]{2,1,0:T(8,128)(2,1)S(1)}, u32[]{:S(2)}, u32[]{:S(2)}) collective-permute-start(bf16[1,768,768]{2,1,0:T(8,128)(2,1)} %all-gather.19.cloned.1.call-done), channel_id=1, source_target_pairs={{0,1},{1,2},{2,3},{3,0},{4,5},{5,6},{6,7},{7,4},{8,9},{9,10},{10,1... | collective-permute-start | bytes 3538952 | tf_op jit(solution)/shard_map/ppermute | solution.py:26
  113.7 67.7 %collective-permute-start.1 = (bf16[1,768,768]{2,1,0:T(8,128)(2,1)S(1)}, bf16[1,768,768]{2,1,0:T(8,128)(2,1)S(1)}, u32[]{:S(2)}, u32[]{:S(2)}) collective-permute-start(bf16[1,768,768]{2,1,0:T(8,128)(2,1)S(1)} %collective-permute-done), channel_id=1, source_target_pairs={{0,1},{1,2},{2,3},{3,0},{4,5},{5,6},{6,7},{7,4},{8,9},{9,10},{10,1... | collective-permute-start | bytes 3538952 | tf_op jit(solution)/shard_map/ppermute | solution.py:26
  132.7 79.1 %copy-start.47 = (f32[128]{0:T(128)}, f32[128]{0:T(128)S(1)}, u32[]{:S(2)}) copy-start(f32[128]{0:T(128)S(1)} %broadcast_multiply_fusion.7) | copy-start | bytes 1540
  181.4 80.8 %collective-permute-start.2 = (bf16[1,768,768]{2,1,0:T(8,128)(2,1)S(1)}, bf16[1,768,768]{2,1,0:T(8,128)(2,1)S(1)}, u32[]{:S(2)}, u32[]{:S(2)}) collective-permute-start(bf16[1,768,768]{2,1,0:T(8,128)(2,1)S(1)} %collective-permute-done.1), channel_id=1, source_target_pairs={{0,1},{1,2},{2,3},{3,0},{4,5},{5,6},{6,7},{7,4},{8,9},{9,10},{10,1... | collective-permute-start | bytes 3538952 | tf_op jit(solution)/shard_map/ppermute | solution.py:26
  271.1 100.0 %copy-start.52 = (f32[128]{0:T(128)}, f32[128]{0:T(128)S(1)}, u32[]{:S(2)}) copy-start(f32[128]{0:T(128)S(1)} %broadcast_multiply_fusion.6) | copy-start | bytes 1540
  271.3 99.8 %copy-start.56 = (f32[128]{0:T(128)}, f32[128]{0:T(128)S(1)}, u32[]{:S(2)}) copy-start(f32[128]{0:T(128)S(1)} %add_rsqrt_fusion) | copy-start | bytes 1540
  271.4 34.7 %copy-start.30 = (bf16[128,768]{1,0:T(8,128)(2,1)}, bf16[128,768]{1,0:T(8,128)(2,1)S(1)}, u32[]{:S(2)}) copy-start(bf16[128,768]{1,0:T(8,128)(2,1)S(1)} %add_convert_fusion) | copy-start | bytes 589828
  271.4 34.8 %copy-start.20 = (f32[128,768]{1,0:T(8,128)S(1)}, f32[128,768]{1,0:T(8,128)}, u32[]{:S(2)}) copy-start(f32[128,768]{1,0:T(8,128)} %param.10) | copy-start | bytes 1179652
  306.1 229.8 %all-gather.25.cloned.1.call-start = ((), (), s32[]{:S(2)}) async-start(), calls=%async_computation.6 | async-start | bytes 3932160 | tf_op jit(solution)/shard_map/all_gather | solution.py:195
  312.0 236.9 %reduce-scatter.3.cloned.1.call-start = ((), (), s32[]{:S(2)}) async-start(), calls=%async_computation.5 | async-start | bytes 2654208 | tf_op jit(solution)/shard_map/reduce_scatter | solution.py:292
  382.0 54.1 %copy-start.13 = (bf16[128,12,64]{0,2,1:T(8,128)(2,1)}, bf16[128,12,64]{0,2,1:T(8,128)(2,1)S(1)}, u32[]{:S(2)}) copy-start(bf16[128,12,64]{0,2,1:T(8,128)(2,1)S(1)} %get-tuple-element.47) | copy-start | bytes 589828
  383.2 82.1 %copy-start.15 = (bf16[12,64,128]{2,1,0:T(8,128)(2,1)}, bf16[12,64,128]{2,1,0:T(8,128)(2,1)S(1)}, u32[]{:S(2)}) copy-start(bf16[12,64,128]{2,1,0:T(8,128)(2,1)S(1)} %convolution_convert_fusion) | copy-start | bytes 589828
  383.2 24.1 %copy-start.28 = (bf16[128,768]{1,0:T(8,128)(2,1)S(1)}, bf16[128,768]{1,0:T(8,128)(2,1)}, u32[]{:S(2)}) copy-start(bf16[128,768]{1,0:T(8,128)(2,1)} %copy.59) | copy-start | bytes 589828
  385.1 111.1 %copy-start.11 = (bf16[128,12,64]{0,2,1:T(8,128)(2,1)}, bf16[128,12,64]{0,2,1:T(8,128)(2,1)S(1)}, u32[]{:S(2)}) copy-start(bf16[128,12,64]{0,2,1:T(8,128)(2,1)S(1)} %get-tuple-element.45) | copy-start | bytes 589828
  385.1 108.6 %copy-start.26 = (bf16[512,768]{1,0:T(8,128)(2,1)S(1)}, bf16[512,768]{1,0:T(8,128)(2,1)}, u32[]{:S(2)}) copy-start(bf16[512,768]{1,0:T(8,128)(2,1)} %all_gather.79) | copy-start | bytes 2359300
  385.1 108.6 %copy-start.27 = (bf16[512,768]{1,0:T(8,128)(2,1)S(1)}, bf16[512,768]{1,0:T(8,128)(2,1)}, u32[]{:S(2)}) copy-start(bf16[512,768]{1,0:T(8,128)(2,1)} %all_gather.78) | copy-start | bytes 2359300
  386.0 79.3 %copy-start.29 = (bf16[128,768]{1,0:T(8,128)(2,1)S(1)}, bf16[128,768]{1,0:T(8,128)(2,1)}, u32[]{:S(2)}) copy-start(bf16[128,768]{1,0:T(8,128)(2,1)} %copy.61) | copy-start | bytes 589828
  496.3 20.9 %copy-start.31 = (bf16[128,768]{1,0:T(8,128)(2,1)S(1)}, bf16[128,768]{1,0:T(8,128)(2,1)}, u32[]{:S(2)}) copy-start(bf16[128,768]{1,0:T(8,128)(2,1)} %copy-done.30) | copy-start | bytes 589828
  496.3 104.6 %reduce-scatter.5.cloned.1.call-start = ((), (), s32[]{:S(2)}) async-start(), calls=%async_computation.8 | async-start | bytes 5308416 | tf_op jit(solution)/shard_map/reduce_scatter | solution.py:293
  540.7 133.2 %all-gather.39.cloned.1.call-start = ((), (), s32[]{:S(2)}) async-start(), calls=%async_computation.14 | async-start | bytes 2654208 | tf_op jit(solution)/shard_map/all_gather | solution.py:233
  545.3 55.6 %copy-start.35 = (f32[2,96,768]{2,1,0:T(8,128)S(1)}, f32[2,96,768]{2,1,0:T(8,128)}, u32[]{:S(2)}) copy-start(f32[2,96,768]{2,1,0:T(8,128)} %param.15) | copy-start | bytes 1769476
  602.9 41.3 %copy-start.5 = (f32[2,96,768]{2,1,0:T(8,128)}, f32[2,96,768]{2,1,0:T(8,128)S(1)}, u32[]{:S(2)}) copy-start(f32[2,96,768]{2,1,0:T(8,128)S(1)} %get-tuple-element.36) | copy-start | bytes 1769476
  644.1 73.2 %all-reduce.5.cloned.1.call-start = ((), (), s32[]{:S(2)}) async-start(), calls=%async_computation.15 | async-start | bytes 1179648 | tf_op jit(solution)/shard_map/psum | solution.py:241
  673.9 45.3 %copy-start.61 = (f32[6]{0:T(128)S(1)}, f32[6]{0:T(128)}, u32[]{:S(2)}) copy-start(f32[6]{0:T(128)} %copy-done.60) | copy-start | bytes 76
  673.9 74.1 %copy-start.4 = (bf16[2,768,768]{2,1,0:T(8,128)(2,1)S(1)}, bf16[2,768,768]{2,1,0:T(8,128)(2,1)}, u32[]{:S(2)}) copy-start(bf16[2,768,768]{2,1,0:T(8,128)(2,1)} %all-gather.39.cloned.1.call-done) | copy-start | bytes 7077892
  677.4 70.5 %all-gather.41.cloned.1.call-start = ((), (), s32[]{:S(2)}) async-start(), calls=%async_computation.16 | async-start | bytes 2654208 | tf_op jit(solution)/shard_map/all_gather | solution.py:246
  719.1 55.3 %all-gather.51.cloned.1.call-start = ((), (), s32[]{:S(2)}) async-start(), calls=%async_computation.23 | async-start | bytes 1327104 | tf_op jit(solution)/shard_map/all_gather | solution.py:232
  722.1 83.5 %all-gather.43.cloned.1.call-start = ((), (), s32[]{:S(2)}) async-start(), calls=%async_computation.17 | async-start | bytes 2654208 | tf_op jit(solution)/shard_map/all_gather | solution.py:233
  751.9 53.7 %copy-start.9 = (bf16[2,96,768]{2,1,0:T(8,128)(2,1)S(1)}, bf16[2,96,768]{2,1,0:T(8,128)(2,1)}, u32[]{:S(2)}) copy-start(bf16[2,96,768]{2,1,0:T(8,128)(2,1)} %get-tuple-element.71) | copy-start | bytes 884740
  752.0 79.5 %all-gather.29.cloned.1.call-start = ((), (), s32[]{:S(2)}) async-start(), calls=%async_computation.9 | async-start | bytes 1327104 | tf_op jit(solution)/shard_map/all_gather | solution.py:245
  776.9 54.5 %copy-start.6 = (bf16[1,768,768]{2,1,0:T(8,128)(2,1)S(1)}, bf16[1,768,768]{2,1,0:T(8,128)(2,1)}, u32[]{:S(2)}) copy-start(bf16[1,768,768]{2,1,0:T(8,128)(2,1)} %all-gather.51.cloned.1.call-done) | copy-start | bytes 3538948
  776.9 54.5 %copy-start.8 = (f32[1,96,768]{2,1,0:T(8,128)S(1)}, f32[1,96,768]{2,1,0:T(8,128)}, u32[]{:S(2)}) copy-start(f32[1,96,768]{2,1,0:T(8,128)} %get-tuple-element.33) | copy-start | bytes 884740
  776.9 54.5 %copy-start.23 = (bf16[96,768]{1,0:T(8,128)(2,1)S(1)}, bf16[96,768]{1,0:T(8,128)(2,1)}, u32[]{:S(2)}) copy-start(bf16[96,768]{1,0:T(8,128)(2,1)} %get-tuple-element.61) | copy-start | bytes 442372
  776.9 96.4 %all-reduce.7.cloned.1.call-start = ((), (), s32[]{:S(2)}) async-start(), calls=%async_computation.18 | async-start | bytes 1179648 | tf_op jit(solution)/shard_map/psum | solution.py:241
  809.0 89.5 %all-gather.31.cloned.1.call-start = ((), (), s32[]{:S(2)}) async-start(), calls=%async_computation.10 | async-start | bytes 1327104 | tf_op jit(solution)/shard_map/all_gather | solution.py:232
  834.1 95.1 %copy-start.3 = (bf16[2,768,768]{2,1,0:T(8,128)(2,1)S(1)}, bf16[2,768,768]{2,1,0:T(8,128)(2,1)}, u32[]{:S(2)}) copy-start(bf16[2,768,768]{2,1,0:T(8,128)(2,1)} %all-gather.43.cloned.1.call-done) | copy-start | bytes 7077892
  834.1 95.0 %all-gather.45.cloned.1.call-start = ((), (), s32[]{:S(2)}) async-start(), calls=%async_computation.19 | async-start | bytes 2654208 | tf_op jit(solution)/shard_map/all_gather | solution.py:246
  875.2 79.7 %all-gather.33.cloned.1.call-start = ((), (), s32[]{:S(2)}) async-start(), calls=%async_computation.11 | async-start | bytes 1327104 | tf_op jit(solution)/shard_map/all_gather | solution.py:245
  901.1 84.4 %all-gather.47.cloned.1.call-start = ((), (), s32[]{:S(2)}) async-start(), calls=%async_computation.20 | async-start | bytes 2654208 | tf_op jit(solution)/shard_map/all_gather | solution.py:233
  933.2 52.4 %copy-start.7 = (bf16[2,96,768]{2,1,0:T(8,128)(2,1)S(1)}, bf16[2,96,768]{2,1,0:T(8,128)(2,1)}, u32[]{:S(2)}) copy-start(bf16[2,96,768]{2,1,0:T(8,128)(2,1)} %get-tuple-element.73) | copy-start | bytes 884740
  933.2 78.2 %all-gather.35.cloned.1.call-start = ((), (), s32[]{:S(2)}) async-start(), calls=%async_computation.12 | async-start | bytes 1327104 | tf_op jit(solution)/shard_map/all_gather | solution.py:232
  958.1 53.3 %copy-start.22 = (bf16[96,768]{1,0:T(8,128)(2,1)S(1)}, bf16[96,768]{1,0:T(8,128)(2,1)}, u32[]{:S(2)}) copy-start(bf16[96,768]{1,0:T(8,128)(2,1)} %get-tuple-element.67) | copy-start | bytes 442372
  958.1 95.2 %all-reduce.9.cloned.1.call-start = ((), (), s32[]{:S(2)}) async-start(), calls=%async_computation.21 | async-start | bytes 1179648 | tf_op jit(solution)/shard_map/psum | solution.py:241
  988.9 66.2 %copy-start.58 = (f32[128]{0:T(128)S(1)}, f32[128]{0:T(128)}, u32[]{:S(2)}) copy-start(f32[128]{0:T(128)} %get-tuple-element.14) | copy-start | bytes 1540
  988.9 66.2 %copy-start.57 = (f32[128]{0:T(128)S(1)}, f32[128]{0:T(128)}, u32[]{:S(2)}) copy-start(f32[128]{0:T(128)} %get-tuple-element.15) | copy-start | bytes 1540
  988.9 66.3 %copy-start.19 = (f32[128,768]{1,0:T(8,128)S(1)}, f32[128,768]{1,0:T(8,128)}, u32[]{:S(2)}) copy-start(f32[128,768]{1,0:T(8,128)} %get-tuple-element.60) | copy-start | bytes 1179652
  988.9 66.3 %copy-start.51 = (f32[128]{0:T(128)S(1)}, f32[128]{0:T(128)}, u32[]{:S(2)}) copy-start(f32[128]{0:T(128)} %copy-done.49) | copy-start | bytes 1540
  988.9 67.2 %copy-start.25 = (bf16[128,3072]{1,0:T(8,128)(2,1)S(1)}, bf16[128,3072]{1,0:T(8,128)(2,1)}, u32[]{:S(2)}) copy-start(bf16[128,3072]{1,0:T(8,128)(2,1)} %get-tuple-element.52) | copy-start | bytes 2359300
  989.0 67.2 %copy-start.53 = (f32[768]{0:T(1024)S(1)}, f32[768]{0:T(1024)}, u32[]{:S(2)}) copy-start(f32[768]{0:T(1024)} %get-tuple-element.19) | copy-start | bytes 9220
  989.0 89.7 %all-gather.37.cloned.1.call-start = ((), (), s32[]{:S(2)}) async-start(), calls=%async_computation.13 | async-start | bytes 1327104 | tf_op jit(solution)/shard_map/all_gather | solution.py:245
  1014.0 95.5 %all-gather.49.cloned.1.call-start = ((), (), s32[]{:S(2)}) async-start(), calls=%async_computation.22 | async-start | bytes 2654208 | tf_op jit(solution)/shard_map/all_gather | solution.py:246
  1056.1 5.6 copy-start.39
  1056.1 22.5 %copy-start.21 = (bf16[96,768]{1,0:T(8,128)(2,1)S(1)}, bf16[96,768]{1,0:T(8,128)(2,1)}, u32[]{:S(2)}) copy-start(bf16[96,768]{1,0:T(8,128)(2,1)} %get-tuple-element.69) | copy-start | bytes 442372
  1061.0 48.5 %copy-start.2 = (bf16[2,768,768]{2,1,0:T(8,128)(2,1)S(1)}, bf16[2,768,768]{2,1,0:T(8,128)(2,1)}, u32[]{:S(2)}) copy-start(bf16[2,768,768]{2,1,0:T(8,128)(2,1)} %all-gather.47.cloned.1.call-done) | copy-start | bytes 7077892
  1061.0 48.5 %copy-start.10 = (f32[2,96,768]{2,1,0:T(8,128)S(1)}, f32[2,96,768]{2,1,0:T(8,128)}, u32[]{:S(2)}) copy-start(f32[2,96,768]{2,1,0:T(8,128)} %get-tuple-element.74) | copy-start | bytes 1769476
  1061.7 51.7 %copy-start.37 = (f32[12,768]{1,0:T(8,128)}, f32[12,768]{1,0:T(8,128)S(1)}, u32[]{:S(2)}) copy-start(f32[12,768]{1,0:T(8,128)S(1)} %get-tuple-element.30) | copy-start | bytes 110596
  (24 other events, 81.0 us)
Sparse Core Ops, SparseCore 0:
  10.5 31.5 all-gather.20
  44.6 23.9 all-gather.18
  70.1 231.3 all-gather.22
  306.3 92.2 all-gather.26
  399.9 99.3 all-gather.24
  502.6 41.0 reduce-scatter.2
  547.1 53.7 reduce-scatter.4
  644.2 29.6 all-gather.38
  677.6 39.6 all-reduce.4
  719.6 28.3 all-gather.40
  750.4 23.9 all-gather.50
  776.7 28.8 all-gather.42
  807.5 23.9 all-gather.28
  833.7 39.6 all-reduce.6
  875.1 23.3 all-gather.30
  900.2 28.8 all-gather.44
  930.9 23.9 all-gather.32
  956.7 28.8 all-gather.46
  987.5 23.9 all-gather.34
  1013.6 39.6 all-reduce.8
  1055.2 23.3 all-gather.36
  1080.5 28.8 all-gather.48
